TPU v7x, 32 devices: a whole 2x2x4 slice. The times are simulated.
32 devices in a mesh: replica: 16 (over z, x, core), shard: 2 (over y).
Axes of the slice: x: 2, y: 2, z: 4, core: 2. Of those that a mesh axis runs over, the one named last changes fastest.
Arguments:
- tokens: bfloat16 [8192, 768], P(('replica', 'shard')), may hold values from -32 to 32
- lengths: int32 [32], P(('replica', 'shard')), may hold values from 1 to 256, 5120 in all
- cotangent: bfloat16 [8192, 768], P(('replica', 'shard')), may hold values from -6 to 6
- w_qkv: bfloat16 [768, 2304], P('shard'), may hold values from -0.14433757 to 0.14433757
- bias_q: bfloat16 [768], P('shard'), may hold values from -3 to 3
- bias_v: bfloat16 [768], P('shard'), may hold values from -3 to 3
- w_out: bfloat16 [768, 768], P('shard'), may hold values from -1.75 to 1.75
- bias_out: bfloat16 [768], P('shard'), may hold values from -3 to 3
- gain_attn: bfloat16 [768], P('shard'), may hold values from 0.5 to 1.5
- shift_attn: bfloat16 [768], P('shard'), may hold values from -3 to 3
- w_in: bfloat16 [768, 3072], P('shard'), may hold values from -0.21875 to 0.21875
- bias_in: bfloat16 [3072], P('shard'), may hold values from -3 to 3
- w_back: bfloat16 [3072, 768], P('shard'), may hold values from -0.109375 to 0.109375
- bias_back: bfloat16 [768], P('shard'), may hold values from -3 to 3
- gain_ffn: bfloat16 [768], P('shard'), may hold values from 0.5 to 1.5
- shift_ffn: bfloat16 [768], P('shard'), may hold values from -3 to 3
Outputs:
- block_out: bfloat16 [8192, 768], P(('replica', 'shard'))
- grad_tokens: float32 [8192, 768], P(('replica', 'shard'))
- grad_w_qkv: float32 [768, 2304], P('shard')
- grad_bias_q: float32 [768], P('shard')
- grad_bias_v: float32 [768], P('shard')
- grad_w_out: float32 [768, 768], P('shard')
- grad_bias_out: float32 [768], P('shard')
- grad_gain_attn: float32 [768], P('shard')
- grad_shift_attn: float32 [768], P('shard')
- grad_w_in: float32 [768, 3072], P('shard')
- grad_bias_in: float32 [3072], P('shard')
- grad_w_back: float32 [3072, 768], P('shard')
- grad_bias_back: float32 [768], P('shard')
- grad_gain_ffn: float32 [768], P('shard')
- grad_shift_ffn: float32 [768], P('shard')
Inputs may be any that keep to these rules, and one draw needn't show every extreme that they name: `lengths`: each sequence has at least one live token; the longest has exactly 256.
All inputs are finite; a program needn't handle non-finite values. No bound on the sum of `lengths` on one device may be relied on, other than what follows from the above.
Results may differ from a plain program's by a relative error of at most 0.012.
The roundings to bfloat16 on the way count: a program that leaves them out, or rounds other values in their place, can miss the bound.
Values may be sent and summed in bfloat16 or wider, within the bound.
A program may use at most 192 MiB of HBM per device.

v0:
```python
import jax
import jax.numpy as jnp
from jax import lax
from jax.sharding import PartitionSpec as P

HEADS = 12
HEAD_DIM = 64


def product(form, left, right):
    return jnp.einsum(form, left, right, preferred_element_type=jnp.float32)


def normalize(hidden):
    average = jnp.mean(hidden, axis=-1, keepdims=True)
    centred = hidden - average
    inv_std = lax.rsqrt(jnp.mean(centred * centred, axis=-1, keepdims=True) + 1e-12)
    return (centred * inv_std, inv_std)


def norm_back(grad_in, normed, inv_std, gain):
    grad_norm = grad_in * gain
    return inv_std * (
        grad_norm
        - jnp.mean(grad_norm, axis=-1, keepdims=True)
        - normed * jnp.mean(grad_norm * normed, axis=-1, keepdims=True)
    )


def gelu_slope(pre):
    return (
        0.5 * (1.0 + lax.erf(pre * 0.7071067811865476))
        + pre * jnp.exp(-0.5 * pre * pre) * 0.3989422804014327
    )


def on_device(
    tokens,
    lengths,
    cotangent,
    w_qkv,
    bias_q,
    bias_v,
    w_out,
    bias_out,
    gain_attn,
    shift_attn,
    w_in,
    bias_in,
    w_back,
    bias_back,
    gain_ffn,
    shift_ffn,
):
    bf16 = jnp.bfloat16
    f32 = jnp.float32
    full = (
        lax.all_gather(w_qkv, "shard", axis=0, tiled=True),
        lax.all_gather(bias_q, "shard", axis=0, tiled=True),
        lax.all_gather(bias_v, "shard", axis=0, tiled=True),
        lax.all_gather(w_out, "shard", axis=0, tiled=True),
        lax.all_gather(bias_out, "shard", axis=0, tiled=True),
        lax.all_gather(gain_attn, "shard", axis=0, tiled=True),
        lax.all_gather(shift_attn, "shard", axis=0, tiled=True),
        lax.all_gather(w_in, "shard", axis=0, tiled=True),
        lax.all_gather(bias_in, "shard", axis=0, tiled=True),
        lax.all_gather(w_back, "shard", axis=0, tiled=True),
        lax.all_gather(bias_back, "shard", axis=0, tiled=True),
        lax.all_gather(gain_ffn, "shard", axis=0, tiled=True),
        lax.all_gather(shift_ffn, "shard", axis=0, tiled=True),
    )
    f_qkv, f_bq, f_bv, f_out, f_bo, f_ga, f_sa, f_in, f_bi, f_back, f_bb, f_gf, f_sf = full
    group = lengths.shape[0]
    span = tokens.shape[0] // group
    width = tokens.shape[1]
    scale = HEAD_DIM ** (-0.5)
    factor = float(tokens.shape[0] * lax.axis_size("replica") * lax.axis_size("shard")) ** (-0.5)
    live = jnp.arange(span, dtype=jnp.int32)[None, :] < lengths[:, None]
    inputs = tokens.reshape(group, span, width)
    qkv = product("bld,de->ble", inputs, f_qkv)
    query = (qkv[..., :width] + f_bq.astype(f32)).astype(bf16).reshape(group, span, HEADS, HEAD_DIM)
    keys = qkv[..., width : 2 * width].astype(bf16).reshape(group, span, HEADS, HEAD_DIM)
    values = (
        (qkv[..., 2 * width :] + f_bv.astype(f32))
        .astype(bf16)
        .reshape(group, span, HEADS, HEAD_DIM)
    )

    def make_scores():
        raw = product("bqhe,bkhe->bhqk", query, keys) * scale
        return jnp.where(live[:, None, None, :], raw, -1000000000.0)

    scores = make_scores()
    top = jnp.max(scores, axis=-1, keepdims=True)
    expo = jnp.exp(scores - top)
    total = jnp.sum(expo, axis=-1, keepdims=True)
    log_total = top + jnp.log(total)
    attend = (expo / total).astype(bf16)
    context = product("bhqk,bkhe->bqhe", attend, values).reshape(group, span, width).astype(bf16)
    resid_one = inputs.astype(f32) + product("bld,de->ble", context, f_out) + f_bo.astype(f32)
    normed_one, inv_one = normalize(resid_one)
    gain_one = f_ga.astype(f32)
    mid = normed_one * gain_one + f_sa.astype(f32)
    mid_b = mid.astype(bf16)
    pre = product("bld,df->blf", mid_b, f_in) + f_bi.astype(f32)
    act = (0.5 * pre * (1.0 + lax.erf(pre * 0.7071067811865476))).astype(bf16)
    resid_two = mid + product("blf,fd->bld", act, f_back) + f_bb.astype(f32)
    normed_two, inv_two = normalize(resid_two)
    gain_two = f_gf.astype(f32)
    block_out = (normed_two * gain_two + f_sf.astype(f32)).astype(bf16)
    again = (
        lax.all_gather(w_qkv, "shard", axis=0, tiled=True),
        lax.all_gather(bias_q, "shard", axis=0, tiled=True),
        lax.all_gather(bias_v, "shard", axis=0, tiled=True),
        lax.all_gather(w_out, "shard", axis=0, tiled=True),
        lax.all_gather(bias_out, "shard", axis=0, tiled=True),
        lax.all_gather(gain_attn, "shard", axis=0, tiled=True),
        lax.all_gather(shift_attn, "shard", axis=0, tiled=True),
        lax.all_gather(w_in, "shard", axis=0, tiled=True),
        lax.all_gather(bias_in, "shard", axis=0, tiled=True),
        lax.all_gather(w_back, "shard", axis=0, tiled=True),
        lax.all_gather(bias_back, "shard", axis=0, tiled=True),
        lax.all_gather(gain_ffn, "shard", axis=0, tiled=True),
        lax.all_gather(shift_ffn, "shard", axis=0, tiled=True),
    )
    b_qkv = again[0]
    b_out = again[3]
    b_in = again[7]
    b_back = again[9]
    grad_out = cotangent.reshape(group, span, width).astype(f32) * live[..., None].astype(f32)
    g_gain_ffn = jnp.sum(grad_out * normed_two, axis=(0, 1))
    g_shift_ffn = jnp.sum(grad_out, axis=(0, 1))
    grad_two = norm_back(grad_out, normed_two, inv_two, gain_two)
    grad_two_b = grad_two.astype(bf16)
    g_w_back = product("blf,bld->fd", act, grad_two_b)
    g_bias_back = jnp.sum(grad_two, axis=(0, 1))
    grad_pre = product("bld,fd->blf", grad_two_b, b_back) * gelu_slope(pre)
    grad_pre_b = grad_pre.astype(bf16)
    g_w_in = product("bld,blf->df", mid_b, grad_pre_b)
    g_bias_in = jnp.sum(grad_pre, axis=(0, 1))
    grad_mid = grad_two + product("blf,df->bld", grad_pre_b, b_in)
    g_gain_attn = jnp.sum(grad_mid * normed_one, axis=(0, 1))
    g_shift_attn = jnp.sum(grad_mid, axis=(0, 1))
    grad_one = norm_back(grad_mid, normed_one, inv_one, gain_one)
    grad_one_b = grad_one.astype(bf16)
    g_w_out = product("bld,ble->de", context, grad_one_b)
    g_bias_out = jnp.sum(grad_one, axis=(0, 1))
    grad_ctx = (
        product("ble,de->bld", grad_one_b, b_out).astype(bf16).reshape(group, span, HEADS, HEAD_DIM)
    )
    weights_again = jnp.exp(make_scores() - log_total)
    weights_b = weights_again.astype(bf16)
    grad_att = product("bqhe,bkhe->bhqk", grad_ctx, values)
    grad_values = product("bhqk,bqhe->bkhe", weights_b, grad_ctx).reshape(group, span, width)
    delta = jnp.sum(weights_again * grad_att, axis=-1, keepdims=True)
    grad_scores = (weights_again * (grad_att - delta) * scale).astype(bf16)
    grad_query = product("bhqk,bkhe->bqhe", grad_scores, keys).reshape(group, span, width)
    grad_keys = product("bhqk,bqhe->bkhe", grad_scores, query).reshape(group, span, width)
    grad_qkv_b = jnp.concatenate([grad_query, grad_keys, grad_values], axis=-1).astype(bf16)
    g_w_qkv = product("bld,ble->de", inputs, grad_qkv_b)
    g_bias_q = jnp.sum(grad_query, axis=(0, 1))
    g_bias_v = jnp.sum(grad_values, axis=(0, 1))
    grad_input = grad_one + product("ble,de->bld", grad_qkv_b, b_qkv)
    shares = (
        lax.psum_scatter(g_w_qkv * factor, "shard", scatter_dimension=0, tiled=True),
        lax.psum_scatter(g_bias_q * factor, "shard", scatter_dimension=0, tiled=True),
        lax.psum_scatter(g_bias_v * factor, "shard", scatter_dimension=0, tiled=True),
        lax.psum_scatter(g_w_out * factor, "shard", scatter_dimension=0, tiled=True),
        lax.psum_scatter(g_bias_out * factor, "shard", scatter_dimension=0, tiled=True),
        lax.psum_scatter(g_gain_attn * factor, "shard", scatter_dimension=0, tiled=True),
        lax.psum_scatter(g_shift_attn * factor, "shard", scatter_dimension=0, tiled=True),
        lax.psum_scatter(g_w_in * factor, "shard", scatter_dimension=0, tiled=True),
        lax.psum_scatter(g_bias_in * factor, "shard", scatter_dimension=0, tiled=True),
        lax.psum_scatter(g_w_back * factor, "shard", scatter_dimension=0, tiled=True),
        lax.psum_scatter(g_bias_back * factor, "shard", scatter_dimension=0, tiled=True),
        lax.psum_scatter(g_gain_ffn * factor, "shard", scatter_dimension=0, tiled=True),
        lax.psum_scatter(g_shift_ffn * factor, "shard", scatter_dimension=0, tiled=True),
    )
    s_qkv, s_bq, s_bv, s_out, s_bo, s_ga, s_sa, s_in, s_bi, s_back, s_bb, s_gf, s_sf = shares
    summed = lax.psum(
        (s_qkv, s_bq, s_bv, s_out, s_bo, s_ga, s_sa, s_in, s_bi, s_back, s_bb, s_gf, s_sf),
        "replica",
    )
    r_qkv, r_bq, r_bv, r_out, r_bo, r_ga, r_sa, r_in, r_bi, r_back, r_bb, r_gf, r_sf = summed
    return (
        block_out.reshape(group * span, width),
        grad_input.reshape(group * span, width),
        r_qkv,
        r_bq,
        r_bv,
        r_out,
        r_bo,
        r_ga,
        r_sa,
        r_in,
        r_bi,
        r_back,
        r_bb,
        r_gf,
        r_sf,
    )


def solution(mesh):
    placed = (
        P(("replica", "shard"), None),
        P(("replica", "shard")),
        P(("replica", "shard"), None),
        P("shard", None),
        P("shard"),
        P("shard"),
        P("shard", None),
        P("shard"),
        P("shard"),
        P("shard"),
        P("shard", None),
        P("shard"),
        P("shard", None),
        P("shard"),
        P("shard"),
        P("shard"),
    )
    return jax.shard_map(
        on_device,
        mesh=mesh,
        in_specs=placed,
        out_specs=(
            P(("replica", "shard"), None),
            P(("replica", "shard"), None),
            P("shard", None),
            P("shard"),
            P("shard"),
            P("shard", None),
            P("shard"),
            P("shard"),
            P("shard"),
            P("shard", None),
            P("shard"),
            P("shard", None),
            P("shard"),
            P("shard"),
            P("shard"),
        ),
        check_vma=False,
    )
```

profile of v0, /device:TPU:0, one launch (start us, length us, event | category | flops | bytes accessed | tf_op | source)
XLA Modules:
  0.0 862.2 jit_solution(6676754043816239792)
XLA Ops:
  10.8 5.3 all-gather.1
  16.2 4.4 all-gather
  20.6 4.4 all-gather.2
  25.0 4.7 all-gather.3
  29.7 4.5 all-gather.4
  34.3 4.5 all-gather.6
  39.4 4.5 all-gather.7
  44.0 4.5 all-gather.8
  49.1 4.6 all-gather.5
  55.5 6.5 all-gather.14.cloned.1.call-done
  62.0 3.1 convolution_bitcast_fusion
  66.2 1.0 copy.55
  68.1 1.9 fusion.63
  71.1 1.4 fusion.34
  72.5 13.8 %all-gather.16.cloned.1.call-done = bf16[768,768]{1,0:T(8,128)(2,1)} async-done(((bf16[384,768]{1,0:T(8,128)(2,1)}), bf16[768,768]{1,0:T(8,128)(2,1)}) %all-gather.16.cloned.1.call-update) | async-done | bytes 1179664 | tf_op jit(solution)/shard_map/all_gather | solution.py:61
  86.3 2.0 fusion.64
  90.0 60.5 %all-gather.18.cloned.1.call-done = bf16[768,3072]{1,0:T(8,128)(2,1)} async-done(((bf16[384,3072]{1,0:T(8,128)(2,1)}), bf16[768,3072]{1,0:T(8,128)(2,1)}) %all-gather.18.cloned.1.call-update) | async-done | bytes 4718608 | tf_op jit(solution)/shard_map/all_gather | solution.py:65
  150.5 6.6 multiply_convert_fusion.1
  157.1 57.5 %all-gather.20.cloned.1.call-done = bf16[3072,768]{1,0:T(8,128)(2,1)} async-done(((bf16[1536,768]{1,0:T(8,128)(2,1)}), bf16[3072,768]{1,0:T(8,128)(2,1)}) %all-gather.20.cloned.1.call-update) | async-done | bytes 4718608 | tf_op jit(solution)/shard_map/all_gather | solution.py:67
  214.6 4.7 fusion.65
  219.5 1.0 multiply_reduce_fusion.1
  220.6 1.7 fusion.59
  222.3 3.0 fusion.68
  225.4 2.2 multiply_reduce_fusion.2
  229.4 1.9 convolution_multiply_fusion.3
  231.6 1.4 log_add_fusion
  232.9 2.8 convolution_convert_fusion
  235.7 1.9 copy.57
  237.6 3.5 fusion.69
  241.1 5.1 fusion.35
  246.2 5.7 fusion.62
  251.9 1.8 fusion.61
  254.4 4.0 multiply_bitcast_fusion
  258.5 1.0 copy-done.2
  260.1 5.2 convolution_multiply_fusion.1
  265.3 1.1 copy-done.7
  267.0 5.1 convolution_multiply_fusion
  272.2 81.9 %reduce-scatter.5.cloned.1.call-done = f32[384,2304]{0,1:T(8,128)} async-done(((f32[768,2304]{0,1:T(8,128)}), f32[384,2304]{0,1:T(8,128)}) %reduce-scatter.5.cloned.1.call-update) | async-done | bytes 3538960 | tf_op jit(solution)/shard_map/reduce_scatter | solution.py:165
  354.1 113.0 %reduce-scatter.9.cloned.1.call-done = f32[384,3072]{1,0:T(8,128)} async-done(((f32[768,3072]{1,0:T(8,128)}), f32[384,3072]{1,0:T(8,128)}) %reduce-scatter.9.cloned.1.call-update) | async-done | bytes 4718608 | tf_op jit(solution)/shard_map/reduce_scatter | solution.py:172
  467.1 113.0 %reduce-scatter.11.cloned.1.call-done = f32[1536,768]{1,0:T(8,128)} async-done(((f32[3072,768]{1,0:T(8,128)}), f32[1536,768]{1,0:T(8,128)}) %reduce-scatter.11.cloned.1.call-update) | async-done | bytes 4718608 | tf_op jit(solution)/shard_map/reduce_scatter | solution.py:174
  582.9 7.5 all-reduce.11
  591.0 62.7 %all-reduce.9 = (f32[384]{0:T(512)}, f32[384]{0:T(512)}, f32[384]{0:T(512)}, f32[384]{0:T(512)}, f32[384]{0:T(512)}, /*index=5*/f32[1536]{0:T(1024)}, f32[384]{0:T(512)}, f32[384]{0:T(512)}, f32[384]{0:T(512)}) all-reduce(f32[384]{0:T(512)S(1)} %dynamic-slice.1, ...), channel_id=1, replica_groups=mesh['replica'=16,'shard'=2] {'replica'}, use_global_device_ids=true, to_apply=%region_15.16 | all-reduce | flops 4608 | bytes 36864 | tf_op jit(solution)/shard_map/psum | solution.py:180
  653.8 4.1 convolution_add_fusion.2
  657.9 183.6 %all-reduce.14.cloned.1.call-done = (f32[384,2304]{0,1:T(8,128)}, f32[384,768]{1,0:T(8,128)}, f32[384,3072]{1,0:T(8,128)}, f32[1536,768]{1,0:T(8,128)}) async-done(((f32[384,2304]{0,1:T(8,128)}, f32[384,768]{1,0:T(8,128)}, f32[384,3072]{1,0:T(8,128)}, f32[1536,768]{1,0:T(8,128)}), (f32[384,2304]{0,1:T(8,128)}, f32[384,768]{1,0:T(8,128)}, f32[384,3072]{1,0:T(8,128)}, ...) | async-done | bytes 14155792 | tf_op jit(solution)/shard_map/psum | solution.py:180
  841.5 5.2 copy.61
  846.8 1.0 copy.71
  847.8 5.7 copy.72
  853.5 2.2 copy.73
  (191 shorter events, 17.1 us)
Async XLA Ops:
  7.2 3.6 copy-start.38
  7.2 8.9 %copy-start.39 = (bf16[384]{0:T(512)(128)(2,1)S(1)}, bf16[384]{0:T(512)(128)(2,1)}, u32[]{:S(2)}) copy-start(bf16[384]{0:T(512)(128)(2,1)} %param.21) | copy-start | bytes 2308
  7.2 13.3 %copy-start.40 = (bf16[384]{0:T(512)(128)(2,1)S(1)}, bf16[384]{0:T(512)(128)(2,1)}, u32[]{:S(2)}) copy-start(bf16[384]{0:T(512)(128)(2,1)} %param.23) | copy-start | bytes 2308
  7.2 17.8 %copy-start.41 = (bf16[384]{0:T(512)(128)(2,1)S(1)}, bf16[384]{0:T(512)(128)(2,1)}, u32[]{:S(2)}) copy-start(bf16[384]{0:T(512)(128)(2,1)} %param.24) | copy-start | bytes 2308
  7.2 22.5 %copy-start.42 = (bf16[384]{0:T(512)(128)(2,1)S(1)}, bf16[384]{0:T(512)(128)(2,1)}, u32[]{:S(2)}) copy-start(bf16[384]{0:T(512)(128)(2,1)} %param.25) | copy-start | bytes 2308
  7.2 54.8 %all-gather.14.cloned.1.call-start = ((), (), s32[]{:S(2)}) async-start(), calls=%async_computation.4 | async-start | bytes 5308416 | tf_op jit(solution)/shard_map/all_gather | solution.py:58
  8.0 26.3 %copy-start.43 = (bf16[384]{0:T(512)(128)(2,1)S(1)}, bf16[384]{0:T(512)(128)(2,1)}, u32[]{:S(2)}) copy-start(bf16[384]{0:T(512)(128)(2,1)} %param.29) | copy-start | bytes 2308
  8.0 31.4 %copy-start.44 = (bf16[384]{0:T(512)(128)(2,1)S(1)}, bf16[384]{0:T(512)(128)(2,1)}, u32[]{:S(2)}) copy-start(bf16[384]{0:T(512)(128)(2,1)} %param.30) | copy-start | bytes 2308
  8.0 36.0 %copy-start.45 = (bf16[384]{0:T(512)(128)(2,1)S(1)}, bf16[384]{0:T(512)(128)(2,1)}, u32[]{:S(2)}) copy-start(bf16[384]{0:T(512)(128)(2,1)} %param.31) | copy-start | bytes 2308
  8.0 41.1 %copy-start.34 = (bf16[1536]{0:T(1024)(128)(2,1)S(1)}, bf16[1536]{0:T(1024)(128)(2,1)}, u32[]{:S(2)}) copy-start(bf16[1536]{0:T(1024)(128)(2,1)} %param.27) | copy-start | bytes 9220
  8.0 54.0 %copy-start.5 = (bf16[256,768]{1,0:T(8,128)(2,1)S(1)}, bf16[256,768]{1,0:T(8,128)(2,1)}, u32[]{:S(2)}) copy-start(bf16[256,768]{1,0:T(8,128)(2,1)} %param.16) | copy-start | bytes 1179652
  8.0 78.3 %all-gather.16.cloned.1.call-start = ((), (), s32[]{:S(2)}) async-start(), calls=%async_computation.5 | async-start | bytes 1769472 | tf_op jit(solution)/shard_map/all_gather | solution.py:61
  8.8 141.8 %all-gather.18.cloned.1.call-start = ((), (), s32[]{:S(2)}) async-start(), calls=%async_computation.6 | async-start | bytes 7077888 | tf_op jit(solution)/shard_map/all_gather | solution.py:65
  9.5 205.1 %all-gather.20.cloned.1.call-start = ((), (), s32[]{:S(2)}) async-start(), calls=%async_computation.7 | async-start | bytes 7077888 | tf_op jit(solution)/shard_map/all_gather | solution.py:67
  10.1 262.1 %reduce-scatter.7.cloned.1.call-start = ((), (), s32[]{:S(2)}) async-start(), calls=%async_computation.9 | async-start | bytes 3538944 | tf_op jit(solution)/shard_map/reduce_scatter | solution.py:168
  68.1 3.0 copy-start.15
  88.3 139.3 %copy-start.23 = (f32[256]{0:T(256)}, f32[256]{0:T(256)S(1)}, u32[]{:S(2)}) copy-start(f32[256]{0:T(256)S(1)} %broadcast_multiply_fusion.14) | copy-start | bytes 3076
  214.6 7.7 slice-start.4
  214.6 4.9 copy-start.12
  214.6 4.9 copy-start.37
  214.6 6.0 copy-start.25
  214.6 7.7 slice-start.5
  219.3 3.0 copy-start.47
  220.6 4.8 slice-start.2
  222.3 3.1 copy-start.6
  222.3 3.0 copy-start.1
  222.3 3.0 copy-start.30
  222.3 3.0 slice-start.3
  225.4 4.0 copy-start.11
  231.3 122.8 %reduce-scatter.5.cloned.1.call-start = ((), (), s32[]{:S(2)}) async-start(), calls=%async_computation.8 | async-start | bytes 10616832 | tf_op jit(solution)/shard_map/reduce_scatter | solution.py:165
  258.4 208.6 %reduce-scatter.9.cloned.1.call-start = ((), (), s32[]{:S(2)}) async-start(), calls=%async_computation.10 | async-start | bytes 14155776 | tf_op jit(solution)/shard_map/reduce_scatter | solution.py:172
  265.3 314.8 %reduce-scatter.11.cloned.1.call-start = ((), (), s32[]{:S(2)}) async-start(), calls=%async_computation.11 | async-start | bytes 14155776 | tf_op jit(solution)/shard_map/reduce_scatter | solution.py:174
  272.1 569.4 %all-reduce.14.cloned.1.call-start = ((), (), s32[]{:S(2)}) async-start(), calls=%async_computation.12 | async-start | bytes 28311552 | tf_op jit(solution)/shard_map/psum | solution.py:180
  580.0 2.6 copy-start.33
  580.0 2.7 copy-start.36
  580.1 2.7 copy-start.26
  580.1 2.7 copy-start.27
  580.1 2.7 copy-start.35
  580.1 2.7 copy-start.28
  580.1 2.7 copy-start.29
  580.1 2.7 copy-start.32
  580.1 73.7 %copy-start.4 = (f32[256,768]{1,0:T(8,128)S(1)}, f32[256,768]{1,0:T(8,128)}, u32[]{:S(2)}) copy-start(f32[256,768]{1,0:T(8,128)} %copy-done.3) | copy-start | bytes 2359300
  580.1 73.7 %copy-start.10 = (bf16[1,256,12,64]{1,3,2,0:T(8,128)(2,1)S(1)}, bf16[1,256,12,64]{1,3,2,0:T(8,128)(2,1)}, u32[]{:S(2)}) copy-start(bf16[1,256,12,64]{1,3,2,0:T(8,128)(2,1)} %copy-done.9) | copy-start | bytes 1179652
  580.1 73.7 %copy-start.18 = (bf16[12,64,256]{2,1,0:T(8,128)(2,1)S(1)}, bf16[12,64,256]{2,1,0:T(8,128)(2,1)}, u32[]{:S(2)}) copy-start(bf16[12,64,256]{2,1,0:T(8,128)(2,1)} %fusion.35) | copy-start | bytes 1179652
  580.1 73.7 %copy-start.20 = (bf16[1,256,12,64]{1,3,2,0:T(8,128)(2,1)S(1)}, bf16[1,256,12,64]{1,3,2,0:T(8,128)(2,1)}, u32[]{:S(2)}) copy-start(bf16[1,256,12,64]{1,3,2,0:T(8,128)(2,1)} %get-tuple-element.100) | copy-start | bytes 1179652
  841.5 5.3 copy-start.16
  846.8 6.7 slice-start
  847.8 5.7 slice-start.1
  (15 other events, 20.7 us)
Sparse Core Ops, SparseCore 0:
  9.6 52.3 all-gather.13
  63.5 22.7 all-gather.15
  87.9 62.6 all-gather.17
  151.9 62.6 all-gather.19
  231.4 34.7 reduce-scatter.6
  268.4 85.6 reduce-scatter.4
  356.4 110.6 reduce-scatter.8
  469.4 110.6 reduce-scatter.10
  584.6 256.8 all-reduce.13
where the time goes:
time: 863 us; the launch traced here: 862 us
  waiting for transfers between devices  632 us (73%)
  blocking collectives  112 us (13%)
  matrix products  64 us (7%)
  local copies, waits for them, and re-layouts  28.7 us (3%)
  between operations  16.4 us (2%)
    psum x1, waiting for transfers between devices, on_device(): lax.psum((s_qkv, s_bq, s_bv, s_out, s_bo, s_ga, s_sa, s_in, s_bi, s_back,...  184 us
    reduce_scatter x1, waiting for transfers between devices, on_device(): lax.psum_scatter(g_w_back * factor, 'shard', scatter_dimension=0, tiled=T...  113 us
    reduce_scatter x1, waiting for transfers between devices, on_device(): lax.psum_scatter(g_w_in * factor, 'shard', scatter_dimension=0, tiled=True)  113 us
    reduce_scatter x1, waiting for transfers between devices, on_device(): lax.psum_scatter(g_w_qkv * factor, 'shard', scatter_dimension=0, tiled=True)  81.9 us
    dot_general x18, matrix products, product(): return jnp.einsum(form, left, right, preferred_element_type=jnp.float32)  64 us
    psum x1, blocking collectives, on_device(): lax.psum((s_qkv, s_bq, s_bv, s_out, s_bo, s_ga, s_sa, s_in, s_bi, s_back,...  62.7 us
    all_gather x1, waiting for transfers between devices, on_device(): lax.all_gather(w_in, 'shard', axis=0, tiled=True)  60.5 us
    all_gather x1, waiting for transfers between devices, on_device(): lax.all_gather(w_back, 'shard', axis=0, tiled=True)  57.5 us
  transfers between devices with their start and end apart: 9, of which 8 were waited for; matrix products, arithmetic and copies ran while one was open for 7% of the time, Pallas kernels for 0%

commit v1 on v0

--- a/solution.py
+++ b/solution.py
@@ -5,6 +5,18 @@
 
 HEADS = 12
 HEAD_DIM = 64
+
+
+def doubled_up(value, axis, dim):
+    ways, here = (lax.axis_size(axis), lax.axis_index(axis))
+    grown, reach = (value, 1)
+    while reach < ways:
+        theirs = lax.ppermute(grown, axis, [(d, d ^ reach) for d in range(ways)])
+        mine_first = jnp.concatenate([grown, theirs], axis=dim)
+        theirs_first = jnp.concatenate([theirs, grown], axis=dim)
+        grown = jnp.where(here & reach == 0, mine_first, theirs_first)
+        reach = 2 * reach
+    return grown
 
 
 def product(form, left, right):
@@ -62,7 +74,7 @@
         lax.all_gather(bias_out, "shard", axis=0, tiled=True),
         lax.all_gather(gain_attn, "shard", axis=0, tiled=True),
         lax.all_gather(shift_attn, "shard", axis=0, tiled=True),
-        lax.all_gather(w_in, "shard", axis=0, tiled=True),
+        doubled_up(w_in, "shard", 0),
         lax.all_gather(bias_in, "shard", axis=0, tiled=True),
         lax.all_gather(w_back, "shard", axis=0, tiled=True),
         lax.all_gather(bias_back, "shard", axis=0, tiled=True),

time: 863 us -> 893 us (1.035)
  blocking collectives: 112 us -> 193 us
  waiting for transfers between devices: 632 us -> 574 us
    all_gather x1, blocking collectives: 5.31 us -> 87.7 us  [on_device(): lax.all_gather(bias_q, 'shard', axis=0, tiled=True)]
    all_gather x1, waiting for transfers between devices: 57.5 us -> 28.8 us  [on_device(): lax.all_gather(w_back, 'shard', axis=0, tiled=True)]
    all_gather x1, waiting for transfers between devices: 13.8 us -> 0.01 us  [on_device(): lax.all_gather(w_out, 'shard', axis=0, tiled=True)]
    unnamed x131 -> x129, local copies, waits for them, and re-layouts: 22.5 us -> 23.1 us
  transfers between devices with their start and end apart: 9 -> 10, of which waited for: 8 -> 6; matrix products, arithmetic and copies ran while one was open for 7% -> 8% of each run, Pallas kernels for 0% -> 0%
where the time goes in v1:
time: 893 us
  waiting for transfers between devices  574 us (64%)
  blocking collectives  193 us (22%)
  matrix products  68.2 us (8%)
  local copies, waits for them, and re-layouts  29.3 us (3%)
  between operations  16.4 us (2%)
    psum x1, waiting for transfers between devices, on_device(): lax.psum((s_qkv, s_bq, s_bv, s_out, s_bo, s_ga, s_sa, s_in, s_bi, s_back,...  184 us
    reduce_scatter x1, waiting for transfers between devices, on_device(): lax.psum_scatter(g_w_in * factor, 'shard', scatter_dimension=0, tiled=True)  113 us
    reduce_scatter x1, waiting for transfers between devices, on_device(): lax.psum_scatter(g_w_back * factor, 'shard', scatter_dimension=0, tiled=T...  113 us
    all_gather x1, blocking collectives, on_device(): lax.all_gather(bias_q, 'shard', axis=0, tiled=True)  87.7 us
    reduce_scatter x1, waiting for transfers between devices, on_device(): lax.psum_scatter(g_w_qkv * factor, 'shard', scatter_dimension=0, tiled=True)  81.9 us
    dot_general x18, matrix products, product(): return jnp.einsum(form, left, right, preferred_element_type=jnp.float32)  68.2 us
    psum x1, blocking collectives, on_device(): lax.psum((s_qkv, s_bq, s_bv, s_out, s_bo, s_ga, s_sa, s_in, s_bi, s_back,...  62.8 us
    all_gather x1, waiting for transfers between devices, on_device(): lax.all_gather(w_in, 'shard', axis=0, tiled=True)  51.8 us
  transfers between devices with their start and end apart: 10, of which 6 were waited for; matrix products, arithmetic and copies ran while one was open for 8% of the time, Pallas kernels for 0%

profile of v1, /device:TPU:0, one launch (start us, length us, event | category | flops | bytes accessed | tf_op | source)
XLA Modules:
  0.0 892.7 jit_solution(7422767984354038672)
XLA Ops:
  9.5 3.1 collective-permute-start
  14.4 87.7 %all-gather.1 = bf16[2,1,384]{2,1,0:T(2,128)(2,1)S(1)} all-gather(bf16[1,1,384]{2,1,0:T(2,128)(2,1)S(1)} %reshape.402), channel_id=1, replica_groups=mesh['replica'=16,'shard'=2] {'shard'}, dimensions={0}, use_global_device_ids=true | all-gather | bytes 2304 | tf_op jit(solution)/shard_map/all_gather | solution.py:71
  102.2 4.4 all-gather
  106.6 4.4 all-gather.2
  111.0 4.5 all-gather.3
  115.6 4.5 all-gather.4
  120.2 4.4 all-gather.6
  125.1 4.3 all-gather.7
  129.5 4.4 all-gather.8
  134.5 4.4 all-gather.5
  139.6 3.1 convolution_bitcast_fusion
  142.9 0.9 copy.54
  143.8 1.0 copy.55
  145.7 1.9 fusion.76
  148.7 1.4 fusion.43
  150.1 2.0 fusion.77
  153.0 6.7 multiply_convert_fusion.1
  159.7 28.8 %all-gather.18.cloned.1.call-done = bf16[3072,768]{1,0:T(8,128)(2,1)} async-done(((bf16[1536,768]{1,0:T(8,128)(2,1)}), bf16[3072,768]{1,0:T(8,128)(2,1)}) %all-gather.18.cloned.1.call-update) | async-done | bytes 4718608 | tf_op jit(solution)/shard_map/all_gather | solution.py:79
  188.4 4.7 fusion.78
  193.4 1.0 multiply_reduce_fusion.1
  194.4 1.7 fusion.72
  197.0 3.7 fusion.81
  200.7 51.8 %all-gather.20.cloned.1.call-done = bf16[768,3072]{1,0:T(8,128)(2,1)} async-done(((bf16[384,3072]{1,0:T(8,128)(2,1)}), bf16[768,3072]{1,0:T(8,128)(2,1)}) %all-gather.20.cloned.1.call-update) | async-done | bytes 4718608 | tf_op jit(solution)/shard_map/all_gather | solution.py:131
  252.5 5.6 multiply_reduce_fusion.2
  259.9 1.9 convolution_multiply_fusion.2
  262.0 1.4 log_add_fusion
  263.4 2.8 convolution_convert_fusion
  266.2 1.9 copy.57
  268.1 3.5 fusion.82
  271.6 5.1 fusion.44
  276.7 5.7 fusion.75
  282.4 1.8 fusion.74
  284.9 4.0 multiply_bitcast_fusion
  288.9 1.0 copy-done.2
  290.5 5.2 convolution_multiply_fusion.1
  295.8 1.1 copy-done.7
  297.5 5.1 convolution_multiply_fusion
  302.7 81.9 %reduce-scatter.5.cloned.1.call-done = f32[384,2304]{0,1:T(8,128)} async-done(((f32[768,2304]{0,1:T(8,128)}), f32[384,2304]{0,1:T(8,128)}) %reduce-scatter.5.cloned.1.call-update) | async-done | bytes 3538960 | tf_op jit(solution)/shard_map/reduce_scatter | solution.py:177
  384.6 113.0 %reduce-scatter.9.cloned.1.call-done = f32[384,3072]{1,0:T(8,128)} async-done(((f32[768,3072]{1,0:T(8,128)}), f32[384,3072]{1,0:T(8,128)}) %reduce-scatter.9.cloned.1.call-update) | async-done | bytes 4718608 | tf_op jit(solution)/shard_map/reduce_scatter | solution.py:184
  497.6 113.0 %reduce-scatter.11.cloned.1.call-done = f32[1536,768]{1,0:T(8,128)} async-done(((f32[3072,768]{1,0:T(8,128)}), f32[1536,768]{1,0:T(8,128)}) %reduce-scatter.11.cloned.1.call-update) | async-done | bytes 4718608 | tf_op jit(solution)/shard_map/reduce_scatter | solution.py:186
  613.3 7.5 all-reduce.11
  621.5 62.8 %all-reduce.9 = (f32[384]{0:T(512)}, f32[384]{0:T(512)}, f32[384]{0:T(512)}, f32[384]{0:T(512)}, f32[384]{0:T(512)}, /*index=5*/f32[1536]{0:T(1024)}, f32[384]{0:T(512)}, f32[384]{0:T(512)}, f32[384]{0:T(512)}) all-reduce(f32[384]{0:T(512)S(1)} %dynamic-slice.1, ...), channel_id=1, replica_groups=mesh['replica'=16,'shard'=2] {'replica'}, use_global_device_ids=true, to_apply=%region_15.16 | all-reduce | flops 4608 | bytes 36864 | tf_op jit(solution)/shard_map/psum | solution.py:192
  684.3 4.1 convolution_add_fusion.1
  688.4 183.5 %all-reduce.14.cloned.1.call-done = (f32[384,2304]{0,1:T(8,128)}, f32[384,768]{1,0:T(8,128)}, f32[384,3072]{1,0:T(8,128)}, f32[1536,768]{1,0:T(8,128)}) async-done(((f32[384,2304]{0,1:T(8,128)}, f32[384,768]{1,0:T(8,128)}, f32[384,3072]{1,0:T(8,128)}, f32[1536,768]{1,0:T(8,128)}), (f32[384,2304]{0,1:T(8,128)}, f32[384,768]{1,0:T(8,128)}, f32[384,3072]{1,0:T(8,128)}, ...) | async-done | bytes 14155792 | tf_op jit(solution)/shard_map/psum | solution.py:192
  872.0 5.2 copy.61
  877.2 1.0 copy.71
  878.3 5.7 copy.72
  884.0 2.2 copy.73
  (190 shorter events, 15.7 us)
Async XLA Ops:
  7.2 7.2 copy-start.39
  7.2 95.0 %copy-start.40 = (bf16[384]{0:T(512)(128)(2,1)S(1)}, bf16[384]{0:T(512)(128)(2,1)}, u32[]{:S(2)}) copy-start(bf16[384]{0:T(512)(128)(2,1)} %param.21) | copy-start | bytes 2308
  7.2 99.4 %copy-start.41 = (bf16[384]{0:T(512)(128)(2,1)S(1)}, bf16[384]{0:T(512)(128)(2,1)}, u32[]{:S(2)}) copy-start(bf16[384]{0:T(512)(128)(2,1)} %param.23) | copy-start | bytes 2308
  7.2 103.8 %copy-start.42 = (bf16[384]{0:T(512)(128)(2,1)S(1)}, bf16[384]{0:T(512)(128)(2,1)}, u32[]{:S(2)}) copy-start(bf16[384]{0:T(512)(128)(2,1)} %param.24) | copy-start | bytes 2308
  7.2 108.3 %copy-start.43 = (bf16[384]{0:T(512)(128)(2,1)S(1)}, bf16[384]{0:T(512)(128)(2,1)}, u32[]{:S(2)}) copy-start(bf16[384]{0:T(512)(128)(2,1)} %param.25) | copy-start | bytes 2308
  7.2 132.3 %all-gather.14.cloned.1.call-start = ((), (), s32[]{:S(2)}) async-start(), calls=%async_computation.4 | async-start | bytes 5308416 | tf_op jit(solution)/shard_map/all_gather | solution.py:70
  8.0 112.2 %copy-start.44 = (bf16[384]{0:T(512)(128)(2,1)S(1)}, bf16[384]{0:T(512)(128)(2,1)}, u32[]{:S(2)}) copy-start(bf16[384]{0:T(512)(128)(2,1)} %param.29) | copy-start | bytes 2308
  8.0 117.2 %copy-start.45 = (bf16[384]{0:T(512)(128)(2,1)S(1)}, bf16[384]{0:T(512)(128)(2,1)}, u32[]{:S(2)}) copy-start(bf16[384]{0:T(512)(128)(2,1)} %param.30) | copy-start | bytes 2308
  8.0 121.5 %copy-start.46 = (bf16[384]{0:T(512)(128)(2,1)S(1)}, bf16[384]{0:T(512)(128)(2,1)}, u32[]{:S(2)}) copy-start(bf16[384]{0:T(512)(128)(2,1)} %param.31) | copy-start | bytes 2308
  8.0 126.5 %copy-start.35 = (bf16[1536]{0:T(1024)(128)(2,1)S(1)}, bf16[1536]{0:T(1024)(128)(2,1)}, u32[]{:S(2)}) copy-start(bf16[1536]{0:T(1024)(128)(2,1)} %param.27) | copy-start | bytes 9220
  8.0 131.6 %copy-start.5 = (bf16[256,768]{1,0:T(8,128)(2,1)S(1)}, bf16[256,768]{1,0:T(8,128)(2,1)}, u32[]{:S(2)}) copy-start(bf16[256,768]{1,0:T(8,128)(2,1)} %param.16) | copy-start | bytes 1179652
  8.0 142.1 %all-gather.16.cloned.1.call-start = ((), (), s32[]{:S(2)}) async-start(), calls=%async_computation.5 | async-start | bytes 1769472 | tf_op jit(solution)/shard_map/all_gather | solution.py:73
  8.8 179.7 %all-gather.18.cloned.1.call-start = ((), (), s32[]{:S(2)}) async-start(), calls=%async_computation.6 | async-start | bytes 7077888 | tf_op jit(solution)/shard_map/all_gather | solution.py:79
  9.5 243.0 %all-gather.20.cloned.1.call-start = ((), (), s32[]{:S(2)}) async-start(), calls=%async_computation.7 | async-start | bytes 7077888 | tf_op jit(solution)/shard_map/all_gather | solution.py:131
  9.5 142.8 %collective-permute-start = (bf16[384,3072]{1,0:T(8,128)(2,1)}, bf16[384,3072]{1,0:T(8,128)(2,1)}, u32[]{:S(2)}, u32[]{:S(2)}) collective-permute-start(bf16[384,3072]{1,0:T(8,128)(2,1)} %param.26), channel_id=1, source_target_pairs={{0,1},{1,0},{2,3},{3,2},{4,5},{5,4},{6,7},{7,6},{8,9},{9,8},{10,11... | collective-permute-start | bytes 7077896 | tf_op jit(solution)/shard_map/ppermute | solution.py:14
  12.6 290.0 %reduce-scatter.7.cloned.1.call-start = ((), (), s32[]{:S(2)}) async-start(), calls=%async_computation.9 | async-start | bytes 3538944 | tf_op jit(solution)/shard_map/reduce_scatter | solution.py:180
  145.7 3.0 copy-start.14
  150.1 2.9 copy-start.33
  152.1 106.0 %copy-start.22 = (f32[256]{0:T(256)}, f32[256]{0:T(256)S(1)}, u32[]{:S(2)}) copy-start(f32[256]{0:T(256)S(1)} %broadcast_multiply_fusion.14) | copy-start | bytes 3076
  188.4 8.6 slice-start.2
  188.4 4.9 copy-start.12
  188.4 4.9 copy-start.38
  188.4 5.9 copy-start.24
  188.4 8.6 slice-start.3
  193.1 3.9 copy-start.48
  197.0 55.5 %copy-start.30 = (f32[256]{0:T(256)S(1)}, f32[256]{0:T(256)}, u32[]{:S(2)}) copy-start(f32[256]{0:T(256)} %copy-done.29) | copy-start | bytes 3076
  252.5 5.6 copy-start.1
  252.5 7.4 copy-start.11
  261.8 122.8 %reduce-scatter.5.cloned.1.call-start = ((), (), s32[]{:S(2)}) async-start(), calls=%async_computation.8 | async-start | bytes 10616832 | tf_op jit(solution)/shard_map/reduce_scatter | solution.py:177
  282.4 2.5 copy-start.18
  288.9 208.7 %reduce-scatter.9.cloned.1.call-start = ((), (), s32[]{:S(2)}) async-start(), calls=%async_computation.10 | async-start | bytes 14155776 | tf_op jit(solution)/shard_map/reduce_scatter | solution.py:184
  295.7 314.8 %reduce-scatter.11.cloned.1.call-start = ((), (), s32[]{:S(2)}) async-start(), calls=%async_computation.11 | async-start | bytes 14155776 | tf_op jit(solution)/shard_map/reduce_scatter | solution.py:186
  302.6 569.4 %all-reduce.14.cloned.1.call-start = ((), (), s32[]{:S(2)}) async-start(), calls=%async_computation.12 | async-start | bytes 28311552 | tf_op jit(solution)/shard_map/psum | solution.py:192
  610.5 2.6 copy-start.34
  610.5 2.7 copy-start.37
  610.5 2.7 copy-start.25
  610.5 2.7 copy-start.26
  610.5 2.7 copy-start.36
  610.6 2.7 copy-start.27
  610.6 2.7 copy-start.28
  610.6 2.7 copy-start.32
  610.6 73.7 %copy-start.4 = (f32[256,768]{1,0:T(8,128)S(1)}, f32[256,768]{1,0:T(8,128)}, u32[]{:S(2)}) copy-start(f32[256,768]{1,0:T(8,128)} %copy-done.3) | copy-start | bytes 2359300
  610.6 73.7 %copy-start.10 = (bf16[1,256,12,64]{1,3,2,0:T(8,128)(2,1)S(1)}, bf16[1,256,12,64]{1,3,2,0:T(8,128)(2,1)}, u32[]{:S(2)}) copy-start(bf16[1,256,12,64]{1,3,2,0:T(8,128)(2,1)} %copy-done.9) | copy-start | bytes 1179652
  610.6 73.7 %copy-start.17 = (bf16[12,64,256]{2,1,0:T(8,128)(2,1)S(1)}, bf16[12,64,256]{2,1,0:T(8,128)(2,1)}, u32[]{:S(2)}) copy-start(bf16[12,64,256]{2,1,0:T(8,128)(2,1)} %fusion.44) | copy-start | bytes 1179652
  610.6 73.7 %copy-start.19 = (bf16[1,256,12,64]{1,3,2,0:T(8,128)(2,1)S(1)}, bf16[1,256,12,64]{1,3,2,0:T(8,128)(2,1)}, u32[]{:S(2)}) copy-start(bf16[1,256,12,64]{1,3,2,0:T(8,128)(2,1)} %get-tuple-element.100) | copy-start | bytes 1179652
  872.0 5.3 copy-start.15
  877.2 6.7 slice-start
  878.3 5.7 slice-start.1
  (15 other events, 17.4 us)
Sparse Core Ops, SparseCore 0:
  9.6 90.0 all-gather.13
  101.2 22.8 all-gather.15
  125.7 62.6 all-gather.17
  189.8 62.6 all-gather.19
  261.9 34.7 reduce-scatter.6
  298.9 85.6 reduce-scatter.4
  386.9 110.6 reduce-scatter.8
  499.9 110.6 reduce-scatter.10
  615.1 256.8 all-reduce.13
